TPU v7x, 256 devices: a whole 4x4x8 slice. The times are simulated.
256 devices in a mesh: dp: 32 (over y, z), vocab: 8 (over x, core).
Axes of the slice: x: 4, y: 4, z: 8, core: 2. Of those that a mesh axis runs over, the one named last changes fastest.
Arguments:
- hidden: bfloat16 [12288, 4096], P('dp'), may hold values from -6 to 6
- head_weight: bfloat16 [4096, 16000], P('dp', 'vocab'), may hold values from -0.09375 to 0.09375
- head_bias: float32 [16000], P('vocab'), may hold values from -3.5 to -1.5
- query_len: int32 [128], P('dp'), may hold values from 8 to 32
- passage_len: int32 [128], P('dp'), may hold values from 16 to 64
- neg_owner: int32 [128, 8], P('dp'), may hold values from 0 to 31, all different within a row; in each aligned block of 4 rows (0 to 3, 4 to 7, ...) at most 2 rows name the same one
- neg_index: int32 [128, 8], P('dp'), may hold values from 0 to 3
- teacher: float32 [128, 8], P('dp'), may hold values from -8 to 8
Outputs:
- margin_error: float32 [128, 8], P('dp')
- hidden_grad: float32 [12288, 4096], P(('dp', 'vocab'))
Inputs may be any that keep to these rules, and one draw needn't show every extreme that they name: `neg_owner`: the 8 negatives of a query have different holders. Among the queries of one index of dp no holder appears more than 2 times, and in some of those blocks one holder appears exactly 2 times.
All inputs are finite; a program needn't handle non-finite values.
Results may differ from a plain program's by a relative error of at most 0.0028.
Values may be sent and summed in bfloat16 or wider, within the bound.
A program may use at most 128 MiB of HBM per device.

v0:
```python
import jax
import jax.numpy as jnp
from jax import lax
from jax.sharding import PartitionSpec as P

LQ = 32
LP = 64


TAU = 0.05


def soft_pool(token_logits, token_mask):
    activation = jnp.log1p(jnp.maximum(token_logits, 0.0))
    weights = jnp.exp(activation / TAU) * token_mask[:, :, None]
    summed = jnp.sum(weights, axis=1)
    valid_count = jnp.sum(token_mask, axis=1)[:, None]
    return (TAU * jnp.log(summed / valid_count), weights / summed[:, None, :])


def lengths_mask(lengths, span):
    return (jnp.arange(span)[None, :] < lengths[:, None]).astype(jnp.float32)


def per_device(
    hidden, head_weight, head_bias, query_len, passage_len, neg_owner, neg_index, teacher
):
    query_count = neg_owner.shape[0]
    neg_count = neg_owner.shape[1]
    owners = lax.axis_size("dp")
    head_full = lax.all_gather(head_weight, "dp", axis=0, tiled=True)
    vocab_width = head_full.shape[1]
    logits = jnp.dot(hidden, head_full, preferred_element_type=jnp.float32) + head_bias[None, :]
    query_tokens = query_count * LQ
    query_rep, query_weights = soft_pool(
        logits[:query_tokens].reshape(query_count, LQ, vocab_width), lengths_mask(query_len, LQ)
    )
    passage_rep, passage_weights = soft_pool(
        logits[query_tokens:].reshape(query_count, LP, vocab_width), lengths_mask(passage_len, LP)
    )
    gathered = lax.all_gather(passage_rep, "dp", axis=0, tiled=True)
    passage_ids = neg_owner * query_count + neg_index
    neg_rows = jnp.take(gathered, passage_ids.reshape(-1), axis=0).reshape(
        query_count, neg_count, vocab_width
    )
    pos_part = jnp.sum(query_rep * passage_rep, axis=1)
    neg_part = jnp.sum(query_rep[:, None, :] * neg_rows, axis=2)
    positive, negative = lax.psum((pos_part, neg_part), "vocab")
    margin_error = positive[:, None] - negative - teacher
    grad_pos = jnp.sum(margin_error, axis=1)
    grad_neg = -margin_error
    query_grad = grad_pos[:, None] * passage_rep + jnp.sum(grad_neg[:, :, None] * neg_rows, axis=1)
    neg_terms = (grad_neg[:, :, None] * query_rep[:, None, :]).reshape(-1, vocab_width)
    scattered = jax.ops.segment_sum(
        neg_terms, passage_ids.reshape(-1), num_segments=owners * query_count
    )
    returned_grad = lax.psum_scatter(scattered, "dp", scatter_dimension=0, tiled=True)
    passage_grad = grad_pos[:, None] * query_rep + returned_grad
    relu_slope = (logits > 0).astype(jnp.float32) / (1.0 + jnp.maximum(logits, 0.0))
    d_query = (query_grad[:, None, :] * query_weights).reshape(-1, vocab_width)
    d_passage = (passage_grad[:, None, :] * passage_weights).reshape(-1, vocab_width)
    logit_grad = (jnp.concatenate([d_query, d_passage], axis=0) * relu_slope).astype(jnp.bfloat16)
    hidden_grad = lax.psum_scatter(
        lax.dot_general(
            logit_grad, head_full, (((1,), (1,)), ((), ())), preferred_element_type=jnp.float32
        ),
        "vocab",
        scatter_dimension=0,
        tiled=True,
    )
    return (margin_error, hidden_grad)


def solution(mesh):
    return jax.shard_map(
        per_device,
        mesh=mesh,
        in_specs=(
            P("dp", None),
            P("dp", "vocab"),
            P("vocab"),
            P("dp"),
            P("dp"),
            P("dp", None),
            P("dp", None),
            P("dp", None),
        ),
        out_specs=(P("dp", None), P(("dp", "vocab"), None)),
        check_vma=False,
    )
```

profile of v0, /device:TPU:1, one launch (start us, length us, event | category | flops | bytes accessed | tf_op | source)
XLA Modules:
  0.0 486.5 jit_solution(886235719207810661)
XLA Ops:
  7.2 0.0 copy-start
  7.2 0.0 all-gather.3.cloned.1.call-start
  7.2 0.7 all-gather.3.cloned.1.call-update
  7.9 0.0 all-reduce.4.cloned.1.call-start
  8.0 0.9 compare_and_fusion
  8.8 0.0 copy-start.7
  8.8 0.1 reshape.191
  8.9 0.7 reshape.204
  9.6 0.6 broadcast_in_dim.13
  10.2 0.8 fusion.22
  11.0 0.8 fusion.21
  11.9 0.7 fusion.18
  12.6 0.7 fusion.19
  13.3 144.3 %all-gather.3.cloned.1.call-done = bf16[4096,2000]{0,1:T(8,128)(2,1)} async-done(((bf16[128,2000]{0,1:T(8,128)(2,1)}), bf16[4096,2000]{0,1:T(8,128)(2,1)}) %all-gather.3.cloned.1.call-update) | async-done | bytes 16384016 | tf_op jit(solution)/shard_map/all_gather | solution.py:31
  157.6 0.0 copy-done
  157.6 12.0 %convolution_add_fusion = f32[384,2000]{0,1:T(8,128)S(1)} fusion(bf16[384,4096]{1,0:T(8,128)(2,1)S(1)} %copy-done, bf16[4096,2000]{0,1:T(8,128)(2,1)} %all-gather.3.cloned.1.call-done, f32[2000]{0:T(1024)} %param.10), kind=kOutput, calls=%fused_computation.4 | convolution fusion | flops 6292224000 | bytes 22609728 | tf_op jit(solution)/shard_map/dot_general | solution.py:33
  169.6 0.0 copy-done.7
  169.6 0.0 copy-start.1
  169.6 1.7 fusion.10
  171.3 0.2 copy-done.1
  171.5 2.2 fusion.3
  173.7 2.6 copy.18
  176.3 2.9 copy.19
  179.2 1.4 multiply_reduce_fusion.1
  180.6 1.9 multiply_reduce_fusion
  182.5 0.2 multiply_reduce_fusion.2
  182.7 0.0 copy-start.3
  182.7 0.6 copy-done.3
  183.3 42.1 %all-gather = f32[32,4,2000]{2,1,0:T(4,128)} all-gather(f32[1,4,2000]{2,1,0:T(4,128)S(1)} %multiply_bitcast_fusion), channel_id=1, replica_groups=mesh['dp'=32,'vocab'=8] {'dp'}, dimensions={0}, use_global_device_ids=true | all-gather | bytes 1056000 | tf_op jit(solution)/shard_map/all_gather | solution.py:41
  225.4 2.6 reshape.212
  228.0 2.0 gather_fusion
  230.0 1.5 fusion.13
  231.4 0.8 reduce_sum.80
  232.2 27.3 %all-reduce.1 = (f32[4,8]{1,0:T(4,128)}, f32[4]{0:T(128)}) all-reduce(f32[4,8]{1,0:T(4,128)S(1)} %reduce_sum.80, f32[4]{0:T(128)S(1)} %get-tuple-element.6), channel_id=1, replica_groups=mesh['dp'=32,'vocab'=8] {'vocab'}, use_global_device_ids=true, to_apply=%region_7.8 | all-reduce | flops 36 | bytes 288 | tf_op jit(solution)/shard_map/psum | solution.py:48
  259.4 1.5 fusion.26
  260.9 0.7 mul.151
  261.6 2.2 scatter_custom_fusion
  263.8 0.0 all-reduce.4.cloned.1.call-update
  263.8 0.2 reduce-scatter.2.cloned.1.call-start
  264.0 0.7 reshape.192
  264.7 0.1 reshape.193
  264.8 1.3 dynamic-slice
  266.7 1.1 div.69
  267.8 2.6 copy.20
  270.4 0.0 copy-done.5
  270.4 1.7 div.72
  272.1 3.0 copy.23
  275.1 0.0 copy-done.8
  275.1 0.2 fusion.15
  275.2 0.0 copy-done.9
  275.2 130.2 %all-reduce.4.cloned.1.call-done = f32[128,2000]{1,0:T(8,128)} async-done(((f32[128,2000]{1,0:T(8,128)}), f32[128,2000]{1,0:T(8,128)}) %all-reduce.4.cloned.1.call-update) | async-done | bytes 1024016
  405.4 0.0 copy-done.4
  405.4 0.9 multiply_add_fusion
  406.3 1.1 mul.145
  407.4 2.6 copy.21
  410.1 1.6 mul.154
  411.7 2.9 copy.24
  414.6 0.0 copy-done.6
  414.6 2.6 divide_multiply_fusion.1
  417.1 0.3 copy-done.2
  417.4 3.3 divide_multiply_fusion
  420.7 12.6 %fusion.4 = f32[384,4096]{1,0:T(8,128)} fusion(bf16[4096,2000]{0,1:T(8,128)(2,1)} %all-gather.3.cloned.1.call-done, f32[256,2000]{0,1:T(8,128)S(1)} %divide_multiply_fusion, f32[128,2000]{0,1:T(8,128)S(1)} %divide_multiply_fusion.1, f32[384,2000]{0,1:T(8,128)S(1)} %copy-done.2), kind=kOutput, calls=%fused_computation.11 | convolution fusion | flops 6297600000 | bytes 28819456 | tf_op jit(solution)/shard_map/dot_general | solution.py:64
  433.3 0.0 reduce-scatter.2.cloned.1.call-update
  433.4 46.6 %reduce-scatter.2.cloned.1.call-done = f32[48,4096]{1,0:T(8,128)} async-done(((f32[384,4096]{1,0:T(8,128)}), f32[48,4096]{1,0:T(8,128)}) %reduce-scatter.2.cloned.1.call-update) | async-done | bytes 786448 | tf_op jit(solution)/shard_map/reduce_scatter | solution.py:63
  (12 shorter events, 0.0 us)
Async XLA Ops:
  7.2 150.4 %copy-start = (bf16[384,4096]{1,0:T(8,128)(2,1)S(1)}, bf16[384,4096]{1,0:T(8,128)(2,1)}, u32[]{:S(2)}) copy-start(bf16[384,4096]{1,0:T(8,128)(2,1)} %param.8) | copy-start | bytes 9437188
  7.2 150.4 %all-gather.3.cloned.1.call-start = ((), (), s32[]{:S(2)}) async-start(), calls=%async_computation.1 | async-start | bytes 16896000 | tf_op jit(solution)/shard_map/all_gather | solution.py:31
  7.9 397.5 %all-reduce.4.cloned.1.call-start = ((), (), s32[]{:S(2)}) async-start(), calls=%async_computation.3 | async-start | bytes 2097152
  8.8 160.8 %copy-start.7 = (pred[4,8]{1,0:T(4,128)(4,1)}, pred[4,8]{1,0:T(4,128)(4,1)S(1)}, u32[]{:S(2)}) copy-start(pred[4,8]{1,0:T(4,128)(4,1)S(1)} %get-tuple-element.9) | copy-start | bytes 100
  169.6 1.9 copy-start.1
  182.7 0.6 copy-start.3
  260.9 9.5 %copy-start.5 = (f32[4,8]{1,0:T(4,128)}, f32[4,8]{1,0:T(4,128)S(1)}, u32[]{:S(2)}) copy-start(f32[4,8]{1,0:T(4,128)S(1)} %get-tuple-element.5) | copy-start | bytes 388
  263.8 216.2 %reduce-scatter.2.cloned.1.call-start = ((), (), s32[]{:S(2)}) async-start(), calls=%async_computation.2 | async-start | bytes 7077888 | tf_op jit(solution)/shard_map/reduce_scatter | solution.py:63
  272.1 3.0 copy-start.8
  272.1 3.1 copy-start.9
  272.1 133.3 %copy-start.4 = (f32[4,2000]{1,0:T(4,128)S(1)}, f32[4,2000]{1,0:T(4,128)}, u32[]{:S(2)}) copy-start(f32[4,2000]{1,0:T(4,128)} %copy-done.3) | copy-start | bytes 96004
  411.7 2.9 copy-start.6
  414.6 2.8 copy-start.2
Sparse Core Ops, SparseCore 0:
  10.5 147.1 all-gather.2
  263.9 141.4 all-reduce.3
  433.5 46.4 reduce-scatter.1
where the time goes:
time: 487 us
  waiting for transfers between devices  322 us (66%)
  blocking collectives  69.3 us (14%)
  local copies, waits for them, and re-layouts  32.5 us (7%)
  matrix products  24.6 us (5%)
  other arithmetic  23.6 us (5%)
  between operations  14.5 us (3%)
    all_gather x1, waiting for transfers between devices, per_device(): head_full = lax.all_gather(head_weight, 'dp', axis=0, tiled=True)  144 us
    unnamed x4, waiting for transfers between devices  131 us
    reduce_scatter x1, waiting for transfers between devices, per_device(): lax.psum_scatter(lax.dot_general(logit_grad, head_full, (((1,), (1,)), ((...  46.6 us
    all_gather x1, blocking collectives, per_device(): gathered = lax.all_gather(passage_rep, 'dp', axis=0, tiled=True)  42.1 us
    psum x1, blocking collectives, per_device(): positive, negative = lax.psum((pos_part, neg_part), 'vocab')  27.3 us
    dot_general x1, matrix products, per_device(): lax.dot_general(logit_grad, head_full, (((1,), (1,)), ((), ())), preferre...  12.6 us
    dot_general x1, matrix products, per_device(): jnp.dot(hidden, head_full, preferred_element_type=jnp.float32)  12 us
  transfers between devices with their start and end apart: 3, of which 3 were waited for; matrix products, arithmetic and copies ran while one was open for 3% of the time, Pallas kernels for 0%

commit v1 on v0

v1 whole, which is shorter than its diff:
```python
import functools

import jax
import jax.numpy as jnp
from jax import lax
from jax.experimental import pallas as pl
from jax.experimental.pallas import tpu as pltpu
from jax.sharding import PartitionSpec as P

NY, NZ, NX = 4, 8, 4
NDP = NY * NZ
LQ, LP, QD, NEG = 32, 64, 4, 8
TOK = QD * (LQ + LP)
D = 4096
KB = D // NDP
VW = 2000
VP = 2048
STREAMS = 4
CW = VP // STREAMS
SUB = 2
SR = KB // SUB
META = VP
RW = VP + 128
CH = 512
NCH = D // CH
ROWS = TOK // 8
SCALE = 2.0**-64
TAU = 0.05
HI = lax.Precision.HIGHEST


def kernel(
    w_hbm, hid_hbm, bias_ref, lens_ref, meta_ref,
    margin_ref, out_ref,
    wf, hid, lg_f, rall, inv_ref, lgrad, sbuf, mt_ref, psum_part, ron, fs, fr, ns, nr,
    ld_sem, rsend, rrecv, zsend, zrecv, ysend, yrecv, vsend, vrecv, osend, orecv, fsend, frecv, nsend, nrecv,
):
    dp = lax.axis_index("dp")
    v = lax.axis_index("vocab")
    y, z = dp // NZ, dp % NZ
    x, c = v // 2, v % 2
    y_up, y_dn = (y + 1) % NY, (y + NY - 1) % NY
    z_up, z_dn = (z + 1) % NZ, (z + NZ - 1) % NZ
    x_up, x_dn, x_far = (x + 1) % NX, (x + NX - 1) % NX, (x + 2) % NX

    def dp_dev(yy, zz):
        return {"dp": yy * NZ + zz}

    def v_dev(xx, cc):
        return {"vocab": xx * 2 + cc}

    def remote(src, dst, ss, rs, dev):
        return pltpu.make_async_remote_copy(
            src_ref=src, dst_ref=dst, send_sem=ss, recv_sem=rs, device_id=dev,
            device_id_type=pl.DeviceIdType.MESH,
        )

    my_rows = pl.ds(pl.multiple_of(dp * KB, KB), KB)
    ld_w = pltpu.make_async_copy(w_hbm, wf.at[my_rows, :], ld_sem.at[0])
    ld_h = pltpu.make_async_copy(hid_hbm, hid, ld_sem.at[1])
    ld_w.start()
    ld_h.start()

    barrier = pltpu.get_barrier_semaphore()
    peers = [dp_dev(y_up, z), dp_dev(y_dn, z), dp_dev(y, z_up), dp_dev(y, z_dn)]
    peers += [{"vocab": (v + i) % (2 * NX)} for i in range(1, 2 * NX)]
    for dev in peers:
        pl.semaphore_signal(barrier, inc=1, device_id=dev, device_id_type=pl.DeviceIdType.MESH)
    ld_w.wait()
    pl.semaphore_wait(barrier, len(peers))

    pos_a = NY * z + (y + z) % NY
    tb = (z + NY * NZ - (NY - 1) * y) % NZ
    pos_b = NY * (y + NY * (tb // NY)) + tb % NY

    def at_a(p):
        b, i = p // NY, p % NY
        return ((i + NY * NZ - b) % NY) * NZ + b

    def at_b(p):
        b, i = p // NY, p % NY
        return (b % NY) * NZ + ((NY - 1) * b + i) % NZ

    pos, at = (pos_a, pos_a, pos_b, pos_b), (at_a, at_a, at_b, at_b)
    sign = (1, -1, 1, -1)
    nxt = [{"dp": at[q]((pos[q] + NDP + sign[q]) % NDP)} for q in range(STREAMS)]

    def origin(q, s):
        return at[q]((pos[q] + 2 * NDP - sign[q] * s) % NDP)

    def ring_copy(q, s, sub):
        rows = pl.ds(pl.multiple_of(origin(q, s) * KB + sub * SR, SR), SR)
        part = wf.at[rows, pl.ds(q * CW, CW)]
        return remote(part, part, rsend.at[q, s, sub], rrecv.at[q, s, sub], nxt[q])

    def arrived(q, s, sub):
        rows = pl.ds(pl.multiple_of(origin(q, s) * KB + sub * SR, SR), SR)
        part = wf.at[rows, pl.ds(q * CW, CW)]
        remote(part, part, rsend.at[q, s - 1, sub], rrecv.at[q, s - 1, sub], nxt[q]).wait_recv()

    for sub in range(SUB):
        for q in range(STREAMS):
            ring_copy(q, 0, sub).start()
    lg_f[...] = jnp.broadcast_to(bias_ref[...], (TOK, VP))
    rall[z, y, :, META:] = meta_ref[...]
    ld_h.wait()

    def mm(q, s1, s2):
        o1 = pl.multiple_of(origin(q, s1) * KB, KB)
        o2 = pl.multiple_of(origin(q, s2) * KB, KB)
        cols = pl.ds(q * CW, CW)
        rhs = jnp.concatenate([wf[pl.ds(o1, KB), cols], wf[pl.ds(o2, KB), cols]], axis=0)
        lhs = jnp.concatenate([hid[:, pl.ds(o1, KB)], hid[:, pl.ds(o2, KB)]], axis=1)
        lg_f[:, cols] += jnp.dot(lhs, rhs, preferred_element_type=jnp.float32)

    def pass_on(s):
        for sub in range(SUB):
            for q in range(STREAMS):
                arrived(q, s, sub)
                ring_copy(q, s, sub).start()

    def ring_body(t, carry):
        pass_on(2 * t + 1)

        @pl.when(t > 0)
        def _():
            mm(0, 2 * t - 1, 2 * t)
            mm(1, 2 * t - 1, 2 * t)

        pass_on(2 * t + 2)

        @pl.when(t > 0)
        def _():
            mm(2, 2 * t - 1, 2 * t)
            mm(3, 2 * t - 1, 2 * t)

        return carry

    lax.fori_loop(0, (NDP - 2) // 2, ring_body, 0)
    for q in range(STREAMS):
        mm(q, NDP - 3, NDP - 2)
    for q in range(STREAMS):
        for sub in range(SUB):
            arrived(q, NDP - 1, sub)
        mm(q, 0, NDP - 1)

    row0 = 0
    for g in range(2 * QD):
        span = LQ if g < QD else LP
        n = lens_ref[g]
        mask = lax.broadcasted_iota(jnp.int32, (span, CW), 0) < n
        count = n.astype(jnp.float32)
        for q in range(STREAMS):
            cols = slice(q * CW, (q + 1) * CW)
            l = lg_f[row0 : row0 + span, cols]
            u = 1.0 + jnp.maximum(l, 0.0)
            u2 = u * u
            u4 = u2 * u2
            u8 = u4 * u4
            u16 = u8 * u8
            u19 = jnp.where(mask, u16 * (u2 * u), 0.0)
            summed = jnp.sum(u19 * u, axis=0, keepdims=True)
            lg_f[row0 : row0 + span, cols] = jnp.where(l > 0.0, u19 * SCALE, 0.0)
            rall[z, y, g : g + 1, cols] = TAU * jnp.log(summed / count)
            inv_ref[g : g + 1, cols] = 1.0 / (summed * SCALE)
        row0 += span

    half = VP // 2
    h1 = pl.ds(0, half)
    h0 = pl.ds(half, RW - half)
    far1 = (pl.ds(0, half // 2), pl.ds(half // 2, half // 2))
    far0 = (pl.ds(half, 512), pl.ds(half + 512, RW - half - 512))
    sends = []

    def go(src, ss, rs, dev):
        cp = remote(src, src, ss, rs, dev)
        cp.start()
        sends.append(cp)

    z_next = (dp_dev(y, z_up), dp_dev(y, z_dn))

    def z_origin(way, d):
        return (z + NZ - d) % NZ if way == 0 else (z + d) % NZ

    def z_ref(kind, way, d):
        zo = z_origin(way, d)
        if kind == 0:
            cols = far0[way] if d == NZ // 2 else h0
            return rall.at[zo, :, :, cols]
        cols = far1[way] if d == NZ // 2 else h1
        return rall.at[zo, y, :, cols]

    def z_send(kind, way, d):
        zo = z_origin(way, d - 1)
        if kind == 0:
            cols = far0[way] if d == NZ // 2 else h0
            src = rall.at[zo, :, :, cols]
        else:
            cols = far1[way] if d == NZ // 2 else h1
            src = rall.at[zo, y, :, cols]
        go(src, zsend.at[kind, way, d - 1], zrecv.at[kind, way, d - 1], z_next[way])

    def z_wait(kind, way, d):
        ref = z_ref(kind, way, d)
        remote(ref, ref, zsend.at[kind, way, d - 1], zrecv.at[kind, way, d - 1], z_next[way]).wait_recv()

    def y_send(slot, zo, cols):
        go(rall.at[zo, y, :, cols], ysend.at[slot, 0], yrecv.at[slot, 0], dp_dev(y_up, z))
        go(rall.at[zo, y, :, cols], ysend.at[slot, 1], yrecv.at[slot, 1], dp_dev(y_dn, z))

    def y_wait(slot, way, zo, cols):
        yo = (y_dn, y_up, (y + 2) % NY)[way]
        ref = rall.at[zo, yo, :, cols]
        remote(ref, ref, ysend.at[slot, way], yrecv.at[slot, way], dp_dev(y_up, z)).wait_recv()

    def y_relay(slot, zo, cols):
        y_wait(slot, 0, zo, cols)
        y_wait(slot, 1, zo, cols)
        odd = zo % 2
        src_y = (y + NY - 1 + 2 * odd) % NY
        dst_y = (y + 1 + 2 * odd) % NY
        go(rall.at[zo, src_y, :, cols], ysend.at[slot, 2], yrecv.at[slot, 2], dp_dev(dst_y, z))

    y_send(NZ, z, h0)
    z_send(1, 0, 1)
    z_send(1, 1, 1)
    y_send(0, z, h1)
    y_relay(NZ, z, h0)
    y_wait(NZ, 2, z, h0)
    z_send(0, 0, 1)
    z_send(0, 1, 1)
    y_relay(0, z, h1)
    order = [(0, z)]
    last = []
    for d in range(1, NZ // 2 + 1):
        fresh = []
        for way in range(2):
            z_wait(1, way, d)
            if d < NZ // 2:
                z_send(1, way, d + 1)
                slot = 2 * d - 1 + way
                y_send(slot, z_origin(way, d), h1)
                fresh.append((slot, z_origin(way, d)))
        if d == NZ // 2:
            y_send(NZ - 1, z_origin(0, d), h1)
            fresh.append((NZ - 1, z_origin(0, d)))
        for way in range(2):
            z_wait(0, way, d)
            if d < NZ // 2:
                z_send(0, way, d + 1)
        for slot, zo in last:
            y_relay(slot, zo, h1)
        last = fresh
        order += fresh
    for slot, zo in last:
        y_relay(slot, zo, h1)
    for slot, zo in order:
        y_wait(slot, 2, zo, h1)

    n_rows = NDP * 8
    reps = rall[:, :, :, 0:VP].reshape(n_rows, VP)
    gram = lax.dot_general(
        reps, reps, (((1,), (1,)), ((), ())), precision=HI, preferred_element_type=jnp.float32
    )
    meta = rall[:, :, :, META:].reshape(n_rows, 128)
    meta_t = meta.T
    row_id = lax.broadcasted_iota(jnp.int32, (n_rows, n_rows), 0).astype(jnp.float32)
    lane_id = lax.broadcasted_iota(jnp.int32, (n_rows, n_rows), 1).astype(jnp.float32)
    for k in range(NEG):
        hit = row_id == meta_t[k : k + 1, :]
        sbuf[v, k : k + 1, :] = jnp.sum(jnp.where(hit, gram, 0.0), axis=0, keepdims=True)
    is_pos = row_id == lane_id + QD
    sbuf[v, NEG : NEG + 1, :] = jnp.sum(jnp.where(is_pos, gram, 0.0), axis=0, keepdims=True)
    sbuf[v, NEG + 1 :, :] = jnp.zeros((16 - NEG - 1, n_rows), jnp.float32)
    for i in range(1, 2 * NX):
        go(sbuf.at[v], vsend.at[i - 1], vrecv.at[i - 1], {"vocab": (v + i) % (2 * NX)})
    for i in range(1, 2 * NX):
        ref = sbuf.at[(v + 2 * NX - i) % (2 * NX)]
        remote(ref, ref, vsend.at[i - 1], vrecv.at[i - 1], {"vocab": (v + i) % (2 * NX)}).wait_recv()
    total = sbuf[0]
    for i in range(1, 2 * NX):
        total = total + sbuf[i]
    lane8 = lax.broadcasted_iota(jnp.int32, (NEG, n_rows), 1)
    margin = total[NEG : NEG + 1, :] - total[0:NEG, :] - meta_t[NEG : 2 * NEG, :]
    margin = jnp.where(lane8 % 8 < QD, margin, 0.0)
    mt_ref[...] = jnp.concatenate([margin, jnp.zeros((120, n_rows), jnp.float32)], axis=0).T
    base = pl.multiple_of((z * NY + y) * 8, 8)
    m_loc = mt_ref[pl.ds(base, 8), :]
    margin_ref[...] = m_loc[0:QD, 0:NEG]

    meta_loc = rall[z, y, :, META:]
    sub_id = (lax.broadcasted_iota(jnp.int32, (8, n_rows), 0) + base).astype(jnp.float32)
    lanes = lax.broadcasted_iota(jnp.int32, (8, n_rows), 1).astype(jnp.float32)
    grad_pos_t = jnp.sum(margin, axis=0, keepdims=True)
    grad_pos_l = jnp.sum(m_loc[:, 0:NEG], axis=1, keepdims=True)
    coef = jnp.where(sub_id == lanes + QD, grad_pos_t, 0.0)
    coef = coef + jnp.where(lanes == sub_id + QD, grad_pos_l, 0.0)
    for k in range(NEG):
        coef = coef - jnp.where(sub_id == meta_t[k : k + 1, :], margin[k : k + 1, :], 0.0)
        coef = coef - jnp.where(lanes == meta_loc[:, k : k + 1], m_loc[:, k : k + 1], 0.0)
    rep_grad = lax.dot_general(
        coef, reps, (((1,), (0,)), ((), ())), precision=HI, preferred_element_type=jnp.float32
    )
    row0 = 0
    for g in range(2 * QD):
        span = LQ if g < QD else LP
        e = lg_f[row0 : row0 + span, :]
        lgrad[row0 : row0 + span, :] = ((e * inv_ref[g : g + 1, :]) * rep_grad[g : g + 1, :]).astype(jnp.bfloat16)
        row0 += span

    other = 1 - c

    def on_copy(n):
        return remote(psum_part.at[n, other], ron.at[n], osend.at[n], orecv.at[n], v_dev(x, other))

    def far_copy(n, way):
        return remote(
            fs.at[n, way], fr.at[n, way], fsend.at[n, way], frecv.at[n, way], v_dev((x_up, x_dn)[way], c)
        )

    def near_copy(n, way):
        return remote(
            ns.at[n, way], nr.at[n, way], nsend.at[n, way], nrecv.at[n, way], v_dev((x_up, x_dn)[way], c)
        )

    hw = CH // 2

    def bwd_body(n, carry):
        @pl.when(n < NCH)
        def _():
            rows = pl.ds(pl.multiple_of(n * CH, CH), CH)
            res = lax.dot_general(
                lgrad[...], wf[rows, :], (((1,), (1,)), ((), ())), preferred_element_type=jnp.float32
            )
            for i in range(2 * NX):
                psum_part[n, i % 2, i // 2] = res[i * ROWS : (i + 1) * ROWS, :]
            on_copy(n).start()

        @pl.when((n >= 1) & (n < NCH + 1))
        def _():
            m = n - 1
            on_copy(m).wait_recv()
            far = psum_part[m, c, x_far] + ron[m, x_far]
            fs[m, 0] = far[:, :hw].astype(jnp.bfloat16)
            fs[m, 1] = far[:, hw:].astype(jnp.bfloat16)
            far_copy(m, 0).start()
            far_copy(m, 1).start()

        @pl.when((n >= 2) & (n < NCH + 2))
        def _():
            m = n - 2
            up = psum_part[m, c, x_up] + ron[m, x_up]
            dn = psum_part[m, c, x_dn] + ron[m, x_dn]
            far_copy(m, 0).wait_recv()
            far_copy(m, 1).wait_recv()
            ns[m, 0, :, :hw] = (up[:, :hw] + fr[m, 0].astype(jnp.float32)).astype(jnp.bfloat16)
            ns[m, 0, :, hw:] = up[:, hw:].astype(jnp.bfloat16)
            ns[m, 1, :, :hw] = dn[:, :hw].astype(jnp.bfloat16)
            ns[m, 1, :, hw:] = (dn[:, hw:] + fr[m, 1].astype(jnp.float32)).astype(jnp.bfloat16)
            near_copy(m, 0).start()
            near_copy(m, 1).start()

        @pl.when(n >= 3)
        def _():
            m = n - 3
            own = psum_part[m, c, x] + ron[m, x]
            near_copy(m, 0).wait_recv()
            near_copy(m, 1).wait_recv()
            cols = pl.ds(pl.multiple_of(m * CH, CH), CH)
            out_ref[:, cols] = own + nr[m, 0].astype(jnp.float32) + nr[m, 1].astype(jnp.float32)

        return carry

    lax.fori_loop(0, NCH + 3, bwd_body, 0)

    for cp in sends:
        cp.wait_send()

    def drain(s, carry):
        for q in range(STREAMS):
            for sub in range(SUB):
                ring_copy(q, s, sub).wait_send()
        return carry

    lax.fori_loop(0, NDP - 1, drain, 0)
    for n in range(NCH):
        on_copy(n).wait_send()
        for way in range(2):
            far_copy(n, way).wait_send()
            near_copy(n, way).wait_send()


def per_device(
    hidden, head_weight, head_bias, query_len, passage_len, neg_owner, neg_index, teacher
):
    w = jnp.pad(head_weight, ((0, 0), (0, VP - VW)))
    bias = jnp.pad(head_bias, (0, VP - VW))[None, :]
    lens = jnp.concatenate([query_len, passage_len])
    ids = ((neg_owner % NZ) * NY + neg_owner // NZ) * 8 + QD + neg_index
    meta = jnp.concatenate([ids.astype(jnp.float32), teacher], axis=1)
    meta = jnp.pad(meta, ((0, 4), (0, 112)), constant_values=-1.0)
    dma = pltpu.SemaphoreType.DMA
    vm = pltpu.VMEM
    f32, bf16 = jnp.float32, jnp.bfloat16
    margin, grad = pl.pallas_call(
        kernel,
        out_shape=(
            jax.ShapeDtypeStruct((QD, NEG), f32),
            jax.ShapeDtypeStruct((ROWS, D), f32),
        ),
        in_specs=[
            pl.BlockSpec(memory_space=pl.ANY),
            pl.BlockSpec(memory_space=pl.ANY),
            pl.BlockSpec(memory_space=pltpu.VMEM),
            pl.BlockSpec(memory_space=pltpu.SMEM),
            pl.BlockSpec(memory_space=pltpu.VMEM),
        ],
        out_specs=(pl.BlockSpec(memory_space=pltpu.VMEM), pl.BlockSpec(memory_space=pltpu.VMEM)),
        scratch_shapes=[
            vm((D, VP), bf16),
            vm((TOK, D), bf16),
            vm((TOK, VP), f32),
            vm((NZ, NY, 8, RW), f32),
            vm((8, VP), f32),
            vm((TOK, VP), bf16),
            vm((2 * NX, 16, NDP * 8), f32),
            vm((NDP * 8, 128), f32),
            vm((NCH, 2, NX, ROWS, CH), f32),
            vm((NCH, NX, ROWS, CH), f32),
            vm((NCH, 2, ROWS, CH // 2), bf16),
            vm((NCH, 2, ROWS, CH // 2), bf16),
            vm((NCH, 2, ROWS, CH), bf16),
            vm((NCH, 2, ROWS, CH), bf16),
            dma((2,)),
            dma((STREAMS, NDP, SUB)),
            dma((STREAMS, NDP, SUB)),
            dma((2, 2, NZ // 2)),
            dma((2, 2, NZ // 2)),
            dma((NZ + 1, 3)),
            dma((NZ + 1, 3)),
            dma((2 * NX - 1,)),
            dma((2 * NX - 1,)),
            dma((NCH,)),
            dma((NCH,)),
            dma((NCH, 2)),
            dma((NCH, 2)),
            dma((NCH, 2)),
            dma((NCH, 2)),
        ],
        compiler_params=pltpu.CompilerParams(
            collective_id=0, has_side_effects=True, vmem_limit_bytes=60 * 1024 * 1024
        ),
    )(w, hidden, bias, lens, meta)
    return margin, grad


def solution(mesh):
    return jax.shard_map(
        per_device,
        mesh=mesh,
        in_specs=(
            P("dp", None),
            P("dp", "vocab"),
            P("vocab"),
            P("dp"),
            P("dp"),
            P("dp", None),
            P("dp", None),
            P("dp", None),
        ),
        out_specs=(P("dp", None), P(("dp", "vocab"), None)),
        check_vma=False,
    )
```

time: 487 us -> 223 us (0.46)
  waiting for transfers between devices: 322 us -> 0 us
  Pallas kernels: 0 us -> 212 us
  blocking collectives: 69.3 us -> 0 us
  local copies, waits for them, and re-layouts: 32.5 us -> 6.67 us
  matrix products: 24.6 us -> 0 us
  other arithmetic: 23.6 us -> 3.31 us
  between operations: 14.5 us -> 0.65 us
    pallas_call x0 -> x1, Pallas kernels: none -> 212 us  [per_device(): pl.pallas_call(kernel, out_shape=(jax.ShapeDtypeStruct((QD, NEG), f32), j...]
    all_gather x1 -> x0, waiting for transfers between devices: 144 us -> none  [per_device(): head_full = lax.all_gather(head_weight, 'dp', axis=0, tiled=True)]
    unnamed x4 -> x0, waiting for transfers between devices: 131 us -> none
    reduce_scatter x1 -> x0, waiting for transfers between devices: 46.6 us -> none  [per_device(): lax.psum_scatter(lax.dot_general(logit_grad, head_full, (((1,), (1,)), ((...]
    all_gather x1 -> x0, blocking collectives: 42.1 us -> none  [per_device(): gathered = lax.all_gather(passage_rep, 'dp', axis=0, tiled=True)]
    psum x1 -> x0, blocking collectives: 27.3 us -> none  [per_device(): positive, negative = lax.psum((pos_part, neg_part), 'vocab')]
    dot_general x2 -> x0, matrix products: 24.6 us -> none  [the longest x1 12.6 us: per_device(): lax.dot_general(logit_grad, head_full, (((1,), (1,)), ((), ())), preferre...]
    mul x5 -> x0, local copies, waits for them, and re-layouts: 8.9 us -> none  [the longest x2 4.52 us: per_device(): passage_grad[:, None, :] * passage_weights]
  transfers between devices with their start and end apart: 3 -> 0, of which waited for: 3 -> 0; matrix products, arithmetic and copies ran while one was open for 3% -> 0% of each run, Pallas kernels for 0% -> 0%
where the time goes in v1:
time: 223 us
  Pallas kernels  212 us (95%)
  local copies, waits for them, and re-layouts  6.67 us (3%)
  other arithmetic  3.31 us (1%)
    pallas_call x1, Pallas kernels, per_device(): pl.pallas_call(kernel, out_shape=(jax.ShapeDtypeStruct((QD, NEG), f32), j...  212 us
    unnamed x3, local copies, waits for them, and re-layouts  4.55 us

profile of v1, /device:TPU:1, one launch (start us, length us, event | category | flops | bytes accessed | tf_op | source)
XLA Modules:
  0.0 222.5 jit_solution(7594958137255156424)
XLA Ops:
  0.6 1.3 pad_add_fusion.lens_ref
  1.9 0.7 fusion.5
  2.6 1.3 select_maximum_fusion.meta_ref
  3.9 1.3 pad.13
  5.2 1.2 copy.10
  6.5 0.8 pad.12.w_hbm
  7.3 211.9 %shard_map.95 = (f32[4,8]{1,0:T(4,128)}, f32[48,4096]{1,0:T(8,128)}) custom-call(bf16[128,2048]{1,0:T(8,128)(2,1)} %pad.12.w_hbm, bf16[384,4096]{1,0:T(8,128)(2,1)} %hid_hbm.1, f32[1,2048]{1,0:T(1,128)} %bitcast.1, s32[8]{0:T(128)} %pad_add_fusion.lens_ref, f32[8,128]{1,0:T(8,128)} %select_maximum_fusion.meta_ref), custom_call_target="tpu_custom_call" | custom-call | tf_op jit(solution)/shard_map/pallas_call | solution.py:405
  219.2 1.2 copy.13
  220.4 2.1 copy.14

commit v2 on v1

v2 whole, which is shorter than its diff:
```python
import functools

import jax
import jax.numpy as jnp
from jax import lax
from jax.experimental import pallas as pl
from jax.experimental.pallas import tpu as pltpu
from jax.sharding import PartitionSpec as P

NY, NZ, NX = 4, 8, 4
NDP = NY * NZ
LQ, LP, QD, NEG = 32, 64, 4, 8
TOK = QD * (LQ + LP)
D = 4096
KB = D // NDP
VW = 2000
VP = 2048
STREAMS = 4
CW = VP // STREAMS
HW = VP // 2
SUB = 4
SR = HW // SUB
FAR = NDP // 2
META = VP
RW = VP + 128
CH = 512
NCH = D // CH
S2, S3, S4 = 2, 5, 8
ROWS = TOK // 8
SCALE = 2.0**-64
TAU = 0.05
HI = lax.Precision.HIGHEST


def rem(a, n):
    return lax.rem(a, jnp.int32(n))


def div(a, n):
    return lax.div(a, jnp.int32(n))


def kernel(
    w_hbm, hid_hbm, bias_ref, qlen_ref, plen_ref, owner_ref, index_ref, teacher_ref,
    margin_ref, out_ref,
    wt, hid, bias_s, lg_f, rall, inv_ref, lgrad, sbuf, mt_ref, psum_part, ron, fs, fr, ns, nr,
    ld_sem, rsend, rrecv, zsend, zrecv, ysend, yrecv, vsend, vrecv, osend, orecv, fsend, frecv, nsend, nrecv,
):
    dp = lax.axis_index("dp")
    v = lax.axis_index("vocab")
    y, z = div(dp, NZ), rem(dp, NZ)
    x, c = div(v, 2), rem(v, 2)
    y_up, y_dn = rem(y + 1, NY), rem(y + NY - 1, NY)
    z_up, z_dn = rem(z + 1, NZ), rem(z + NZ - 1, NZ)
    x_up, x_dn, x_far = rem(x + 1, NX), rem(x + NX - 1, NX), rem(x + 2, NX)

    def dp_dev(yy, zz):
        return {"dp": yy * NZ + zz}

    def v_dev(xx, cc):
        return {"vocab": xx * 2 + cc}

    def remote(src, dst, ss, rs, dev):
        return pltpu.make_async_remote_copy(
            src_ref=src, dst_ref=dst, send_sem=ss, recv_sem=rs, device_id=dev,
            device_id_type=pl.DeviceIdType.MESH,
        )

    ld_w = pltpu.make_async_copy(w_hbm, wt.at[dp, 0:VW, :], ld_sem.at[0])
    ld_h = pltpu.make_async_copy(hid_hbm, hid, ld_sem.at[1])
    ld_w.start()
    ld_h.start()

    barrier = pltpu.get_barrier_semaphore()
    peers = [dp_dev(y_up, z), dp_dev(y_dn, z), dp_dev(y, z_up), dp_dev(y, z_dn)]
    peers += [{"vocab": rem(v + i, 2 * NX)} for i in range(1, 2 * NX)]
    for dev in peers:
        pl.semaphore_signal(barrier, inc=1, device_id=dev, device_id_type=pl.DeviceIdType.MESH)
    ld_w.wait()
    pl.semaphore_wait(barrier, len(peers))

    pos_a = NY * z + rem(y + z, NY)
    tb = rem(z + NY * NZ - (NY - 1) * y, NZ)
    pos_b = NY * (y + NY * div(tb, NY)) + rem(tb, NY)

    def at_a(p):
        b, i = div(p, NY), rem(p, NY)
        return rem(i + NY * NZ - b, NY) * NZ + b

    def at_b(p):
        b, i = div(p, NY), rem(p, NY)
        return rem(b, NY) * NZ + rem((NY - 1) * b + i, NZ)

    pos, at = (pos_a, pos_a, pos_b, pos_b), (at_a, at_a, at_b, at_b)
    sign = (1, -1, 1, -1)
    nxt = [{"dp": at[q](rem(pos[q] + NDP + sign[q], NDP))} for q in range(STREAMS)]

    def origin(q, s):
        return at[q](rem(pos[q] + 2 * NDP - sign[q] * s, NDP))

    def ring_copy(q, org, s, sub):
        part = wt.at[org, pl.ds((q // 2) * HW + sub * SR, sub_rows(q, sub)), :]
        return remote(part, part, rsend.at[q, sub], rrecv.at[q, s, sub], nxt[q])

    def sub_rows(q, sub):
        return SR if q < 2 or sub < SUB - 1 else VW - (VP - SR)

    def far_subs(q):
        return range(0, SUB // 2) if q % 2 == 0 else range(SUB // 2, SUB)

    for sub in range(SUB):
        for q in range(STREAMS):
            ring_copy(q, dp, 0, sub).start()

    def clear(i, carry):
        wt[i, VW:, :] = jnp.zeros((VP - VW, KB), jnp.bfloat16)
        return carry

    lax.fori_loop(0, NDP, clear, 0)
    bias_s[...] = jnp.zeros_like(bias_s)
    bias_s[:, 0:VW] = bias_ref[...]
    lg_f[...] = jnp.broadcast_to(bias_s[...], (TOK, VP))
    owner = owner_ref[...]
    ids = (rem(owner, NZ) * NY + div(owner, NZ)) * 8 + QD + index_ref[...]
    rall[z, y, :, META:] = jnp.zeros((8, 128), jnp.float32)
    rall[z, y, 0:QD, META : META + NEG] = ids.astype(jnp.float32)
    rall[z, y, QD:8, META : META + NEG] = teacher_ref[...]
    ld_h.wait()

    def mm(q, o1, o2):
        cols = slice(q * CW, (q + 1) * CW)
        k1 = pl.ds(pl.multiple_of(o1 * KB, KB), KB)
        k2 = pl.ds(pl.multiple_of(o2 * KB, KB), KB)
        rhs = jnp.concatenate([wt[o1, cols, :], wt[o2, cols, :]], axis=1)
        lhs = jnp.concatenate([hid[:, k1], hid[:, k2]], axis=1)
        lg_f[:, cols] += lax.dot_general(
            lhs, rhs, (((1,), (1,)), ((), ())), preferred_element_type=jnp.float32
        )

    def mm_after(sub, org):
        mm(sub, org[sub // 2 * 2], org[sub // 2 * 2 + 1])

    def ring_body(s, before):
        org = [origin(q, s) for q in range(STREAMS)]
        for sub in range(SUB):
            for q in range(STREAMS):
                ring_copy(q, org[q], s - 1, sub).wait_recv()
                if sub in far_subs(q):
                    ring_copy(q, org[q], s, sub).start()
                else:

                    @pl.when(s < FAR - 1)
                    def _():
                        ring_copy(q, org[q], s, sub).start()

            @pl.when(s > 1)
            def _():
                mm_after(sub, before)

        return tuple(org)

    before = lax.fori_loop(1, FAR, ring_body, (dp,) * STREAMS)
    for sub in range(SUB):
        mm_after(sub, before)
    for q in range(STREAMS):
        for sub in far_subs(q):
            ring_copy(q, origin(q, FAR), FAR - 1, sub).wait_recv()
    for q in range(STREAMS):
        mm(q, dp, origin(q // 2 * 2, FAR))

    row0 = 0
    for g in range(2 * QD):
        span = LQ if g < QD else LP
        n = qlen_ref[g] if g < QD else plen_ref[g - QD]
        mask = lax.broadcasted_iota(jnp.int32, (span, CW), 0) < n
        count = n.astype(jnp.float32)
        for q in range(STREAMS):
            cols = slice(q * CW, (q + 1) * CW)
            l = lg_f[row0 : row0 + span, cols]
            u = 1.0 + jnp.maximum(l, 0.0)
            u2 = u * u
            u4 = u2 * u2
            u8 = u4 * u4
            u16 = u8 * u8
            u19 = jnp.where(mask, u16 * (u2 * u), 0.0)
            summed = jnp.sum(u19 * u, axis=0, keepdims=True)
            lg_f[row0 : row0 + span, cols] = jnp.where(l > 0.0, u19 * SCALE, 0.0)
            rall[z, y, g : g + 1, cols] = TAU * jnp.log(summed / count)
            inv_ref[g : g + 1, cols] = 1.0 / (summed * SCALE)
        row0 += span

    half = 1280
    h1 = pl.ds(0, half)
    h0 = pl.ds(half, RW - half)
    far1 = (pl.ds(0, 640), pl.ds(640, half - 640))
    far0 = (pl.ds(half, 384), pl.ds(half + 384, RW - half - 384))
    sends = []

    def go(src, ss, rs, dev):
        cp = remote(src, src, ss, rs, dev)
        cp.start()
        sends.append(cp)

    z_next = (dp_dev(y, z_up), dp_dev(y, z_dn))
    y_off = [y, y_dn, y_up, rem(y + 2, NY)]
    mid = NZ // 2

    def z_origin(way, d):
        return rem(z + NZ - d, NZ) if way == 0 else rem(z + d, NZ)

    def z_copy(j, way, d, zo):
        if j < NY:
            ref = rall.at[zo, y_off[j], :, far0[way] if d == mid else h0]
        else:
            ref = rall.at[zo, y, :, far1[way] if d == mid else h1]
        return remote(ref, ref, zsend.at[j, way, d - 1], zrecv.at[j, way, d - 1], z_next[way])

    def z_send(j, way, d):
        cp = z_copy(j, way, d, z_origin(way, d - 1))
        cp.start()
        sends.append(cp)

    def z_wait(j, way, d):
        z_copy(j, way, d, z_origin(way, d)).wait_recv()

    def y_send(slot, zo, cols):
        go(rall.at[zo, y, :, cols], ysend.at[slot, 0], yrecv.at[slot, 0], dp_dev(y_up, z))
        go(rall.at[zo, y, :, cols], ysend.at[slot, 1], yrecv.at[slot, 1], dp_dev(y_dn, z))

    def y_wait(slot, way, zo, cols):
        ref = rall.at[zo, y_off[way + 1], :, cols]
        remote(ref, ref, ysend.at[slot, way], yrecv.at[slot, way], dp_dev(y_up, z)).wait_recv()

    def y_relay(slot, zo, cols):
        y_wait(slot, 0, zo, cols)
        y_wait(slot, 1, zo, cols)
        odd = rem(zo, 2)
        src_y = rem(y + NY - 1 + 2 * odd, NY)
        dst_y = rem(y + 1 + 2 * odd, NY)
        go(rall.at[zo, src_y, :, cols], ysend.at[slot, 2], yrecv.at[slot, 2], dp_dev(dst_y, z))

    y_send(NZ, z, h0)
    for way in range(2):
        z_send(0, way, 1)
        z_send(NY, way, 1)
    y_send(0, z, h1)
    y_relay(NZ, z, h0)
    for way in range(2):
        z_send(1, way, 1)
        z_send(2, way, 1)
    y_wait(NZ, 2, z, h0)
    for way in range(2):
        z_send(3, way, 1)
    last = [(0, z)]
    order = [(0, z)]
    for d in range(1, mid + 1):
        fresh = []
        for j in (0, NY, 1, 2, 3):
            for way in range(2):
                z_wait(j, way, d)
                if d < mid:
                    z_send(j, way, d + 1)
                if j == NY and (d < mid or way == 1):
                    slot = 2 * d - 1 + way if d < mid else NZ - 1
                    y_send(slot, z_origin(way, d), h1)
                    fresh.append((slot, z_origin(way, d)))
            if j == 1:
                for slot, zo in last:
                    y_relay(slot, zo, h1)
        last = fresh
        order += fresh
    for slot, zo in last:
        y_relay(slot, zo, h1)
    for slot, zo in order:
        y_wait(slot, 2, zo, h1)

    n_rows = NDP * 8
    reps = rall[:, :, :, 0:VP].reshape(n_rows, VP)
    gram = lax.dot_general(
        reps, reps, (((1,), (1,)), ((), ())), precision=HI, preferred_element_type=jnp.float32
    )
    meta = rall[:, :, :, META:].reshape(n_rows, 128)
    meta_t = meta.T
    row_id = lax.broadcasted_iota(jnp.int32, (n_rows, n_rows), 0).astype(jnp.float32)
    lane_id = lax.broadcasted_iota(jnp.int32, (n_rows, n_rows), 1).astype(jnp.float32)
    for k in range(NEG):
        hit = row_id == meta_t[k : k + 1, :]
        sbuf[v, k : k + 1, :] = jnp.sum(jnp.where(hit, gram, 0.0), axis=0, keepdims=True)
    is_pos = row_id == lane_id + QD
    sbuf[v, NEG : NEG + 1, :] = jnp.sum(jnp.where(is_pos, gram, 0.0), axis=0, keepdims=True)
    sbuf[v, NEG + 1 :, :] = jnp.zeros((16 - NEG - 1, n_rows), jnp.float32)
    for i in range(1, 2 * NX):
        go(sbuf.at[v], vsend.at[i - 1], vrecv.at[i - 1], {"vocab": rem(v + i, 2 * NX)})
    for i in range(1, 2 * NX):
        ref = sbuf.at[rem(v + 2 * NX - i, 2 * NX)]
        remote(ref, ref, vsend.at[i - 1], vrecv.at[i - 1], {"vocab": rem(v + i, 2 * NX)}).wait_recv()
    total = sbuf[0]
    for i in range(1, 2 * NX):
        total = total + sbuf[i]
    lane8 = lax.broadcasted_iota(jnp.int32, (NEG, n_rows), 1)
    teacher_t = pltpu.roll(meta_t[0:NEG, :], n_rows - QD, 1)
    margin = total[NEG : NEG + 1, :] - total[0:NEG, :] - teacher_t
    margin = jnp.where(rem(lane8, 8) < QD, margin, 0.0)
    mt_ref[...] = jnp.concatenate([margin, jnp.zeros((120, n_rows), jnp.float32)], axis=0).T
    base = pl.multiple_of((z * NY + y) * 8, 8)
    m_loc = mt_ref[pl.ds(base, 8), :]
    margin_ref[...] = m_loc[0:QD, 0:NEG]

    meta_loc = rall[z, y, :, META:]
    sub_id = (lax.broadcasted_iota(jnp.int32, (8, n_rows), 0) + base).astype(jnp.float32)
    lanes = lax.broadcasted_iota(jnp.int32, (8, n_rows), 1).astype(jnp.float32)
    grad_pos_t = jnp.sum(margin, axis=0, keepdims=True)
    grad_pos_l = jnp.sum(m_loc[:, 0:NEG], axis=1, keepdims=True)
    coef = jnp.where(sub_id == lanes + QD, grad_pos_t, 0.0)
    coef = coef + jnp.where(lanes == sub_id + QD, grad_pos_l, 0.0)
    for k in range(NEG):
        coef = coef - jnp.where(sub_id == meta_t[k : k + 1, :], margin[k : k + 1, :], 0.0)
        coef = coef - jnp.where(lanes == meta_loc[:, k : k + 1], m_loc[:, k : k + 1], 0.0)
    rep_grad = lax.dot_general(
        coef, reps, (((1,), (0,)), ((), ())), precision=HI, preferred_element_type=jnp.float32
    )
    row0 = 0
    for g in range(2 * QD):
        span = LQ if g < QD else LP
        e = lg_f[row0 : row0 + span, :]
        lgrad[row0 : row0 + span, :] = ((e * inv_ref[g : g + 1, :]) * rep_grad[g : g + 1, :]).astype(jnp.bfloat16)
        row0 += span

    other = 1 - c

    def on_copy(n):
        return remote(psum_part.at[n, other], ron.at[n], osend.at[n], orecv.at[n], v_dev(x, other))

    def far_copy(n, way):
        return remote(
            fs.at[n, way], fr.at[n, way], fsend.at[n, way], frecv.at[n, way], v_dev((x_up, x_dn)[way], c)
        )

    def near_copy(n, way):
        return remote(
            ns.at[n, way], nr.at[n, way], nsend.at[n, way], nrecv.at[n, way], v_dev((x_up, x_dn)[way], c)
        )

    hw = CH // 2

    def bwd_body(n, carry):
        @pl.when(n < NCH)
        def _():
            rhs = jnp.concatenate([wt[n * (CH // KB) + i] for i in range(CH // KB)], axis=1)
            res = jnp.dot(lgrad[...], rhs, preferred_element_type=jnp.float32)
            for i in range(2 * NX):
                psum_part[n, i % 2, i // 2] = res[i * ROWS : (i + 1) * ROWS, :]
            on_copy(n).start()

        @pl.when((n >= S2) & (n < NCH + S2))
        def _():
            m = n - S2
            on_copy(m).wait_recv()
            far = psum_part[m, c, x_far] + ron[m, x_far]
            fs[m, 0] = far[:, :hw].astype(jnp.bfloat16)
            fs[m, 1] = far[:, hw:].astype(jnp.bfloat16)
            far_copy(m, 0).start()
            far_copy(m, 1).start()

        @pl.when((n >= S3) & (n < NCH + S3))
        def _():
            m = n - S3
            up = psum_part[m, c, x_up] + ron[m, x_up]
            dn = psum_part[m, c, x_dn] + ron[m, x_dn]
            far_copy(m, 0).wait_recv()
            far_copy(m, 1).wait_recv()
            ns[m, 0, :, :hw] = (up[:, :hw] + fr[m, 0].astype(jnp.float32)).astype(jnp.bfloat16)
            ns[m, 0, :, hw:] = up[:, hw:].astype(jnp.bfloat16)
            ns[m, 1, :, :hw] = dn[:, :hw].astype(jnp.bfloat16)
            ns[m, 1, :, hw:] = (dn[:, hw:] + fr[m, 1].astype(jnp.float32)).astype(jnp.bfloat16)
            near_copy(m, 0).start()
            near_copy(m, 1).start()

        @pl.when(n >= S4)
        def _():
            m = n - S4
            own = psum_part[m, c, x] + ron[m, x]
            near_copy(m, 0).wait_recv()
            near_copy(m, 1).wait_recv()
            cols = pl.ds(pl.multiple_of(m * CH, CH), CH)
            out_ref[:, cols] = own + nr[m, 0].astype(jnp.float32) + nr[m, 1].astype(jnp.float32)

        return carry

    lax.fori_loop(0, NCH + S4, bwd_body, 0)

    for cp in sends:
        cp.wait_send()

    for q in range(STREAMS):
        for sub in range(SUB):
            steps = FAR if sub in far_subs(q) else FAR - 1
            sent = wt.at[0:steps, 0 : sub_rows(q, sub), :]
            remote(sent, sent, rsend.at[q, sub], rrecv.at[q, 0, sub], nxt[q]).wait_send()
    for n in range(NCH):
        on_copy(n).wait_send()
        for way in range(2):
            far_copy(n, way).wait_send()
            near_copy(n, way).wait_send()


def per_device(
    hidden, head_weight, head_bias, query_len, passage_len, neg_owner, neg_index, teacher
):
    dma = pltpu.SemaphoreType.DMA
    vm = pltpu.VMEM
    f32, bf16 = jnp.float32, jnp.bfloat16
    margin, grad = pl.pallas_call(
        kernel,
        out_shape=(
            jax.ShapeDtypeStruct((QD, NEG), f32),
            jax.ShapeDtypeStruct((ROWS, D), f32),
        ),
        in_specs=[
            pl.BlockSpec(memory_space=pl.ANY),
            pl.BlockSpec(memory_space=pl.ANY),
            pl.BlockSpec(memory_space=pltpu.VMEM),
            pl.BlockSpec(memory_space=pltpu.SMEM),
            pl.BlockSpec(memory_space=pltpu.SMEM),
            pl.BlockSpec(memory_space=pltpu.VMEM),
            pl.BlockSpec(memory_space=pltpu.VMEM),
            pl.BlockSpec(memory_space=pltpu.VMEM),
        ],
        out_specs=(pl.BlockSpec(memory_space=pltpu.VMEM), pl.BlockSpec(memory_space=pltpu.VMEM)),
        scratch_shapes=[
            vm((NDP, VP, KB), bf16),
            vm((TOK, D), bf16),
            vm((1, VP), f32),
            vm((TOK, VP), f32),
            vm((NZ, NY, 8, RW), f32),
            vm((8, VP), f32),
            vm((TOK, VP), bf16),
            vm((2 * NX, 16, NDP * 8), f32),
            vm((NDP * 8, 128), f32),
            vm((NCH, 2, NX, ROWS, CH), f32),
            vm((NCH, NX, ROWS, CH), f32),
            vm((NCH, 2, ROWS, CH // 2), bf16),
            vm((NCH, 2, ROWS, CH // 2), bf16),
            vm((NCH, 2, ROWS, CH), bf16),
            vm((NCH, 2, ROWS, CH), bf16),
            dma((2,)),
            dma((STREAMS, SUB)),
            dma((STREAMS, FAR, SUB)),
            dma((NY + 1, 2, NZ // 2)),
            dma((NY + 1, 2, NZ // 2)),
            dma((NZ + 1, 3)),
            dma((NZ + 1, 3)),
            dma((2 * NX - 1,)),
            dma((2 * NX - 1,)),
            dma((NCH,)),
            dma((NCH,)),
            dma((NCH, 2)),
            dma((NCH, 2)),
            dma((NCH, 2)),
            dma((NCH, 2)),
        ],
        compiler_params=pltpu.CompilerParams(
            collective_id=0, has_side_effects=True, vmem_limit_bytes=60 * 1024 * 1024
        ),
    )(
        head_weight.T, hidden, head_bias[None, :], query_len, passage_len, neg_owner, neg_index, teacher
    )
    return margin, grad


def solution(mesh):
    return jax.shard_map(
        per_device,
        mesh=mesh,
        in_specs=(
            P("dp", None),
            P("dp", "vocab"),
            P("vocab"),
            P("dp"),
            P("dp"),
            P("dp", None),
            P("dp", None),
            P("dp", None),
        ),
        out_specs=(P("dp", None), P(("dp", "vocab"), None)),
        check_vma=False,
    )
```

time: 223 us -> 166 us (0.74)
  Pallas kernels: 212 us -> 162 us
  local copies, waits for them, and re-layouts: 6.67 us -> 3.32 us
  other arithmetic: 3.31 us -> 0 us
    pallas_call x1, Pallas kernels: 212 us -> 162 us  [per_device(): pl.pallas_call(kernel, out_shape=(jax.ShapeDtypeStruct((QD, NEG), f32), j...]
    concatenate x2 -> x0, other arithmetic: 2.6 us -> none  [the longest x1 1.35 us: per_device(): meta = jnp.concatenate([ids.astype(jnp.float32), teacher], axis=1)]
    unnamed x3 -> x2, local copies, waits for them, and re-layouts: 4.55 us -> 3.32 us
where the time goes in v2:
time: 166 us
  Pallas kernels  162 us (98%)
  local copies, waits for them, and re-layouts  3.32 us (2%)
    pallas_call x1, Pallas kernels, per_device(): pl.pallas_call(kernel, out_shape=(jax.ShapeDtypeStruct((QD, NEG), f32), j...  162 us

profile of v2, /device:TPU:1, one launch (start us, length us, event | category | flops | bytes accessed | tf_op | source)
XLA Modules:
  0.0 166.2 jit_solution(2928841736067760432)
XLA Ops:
  0.6 162.3 %shard_map.95 = (f32[4,8]{1,0:T(4,128)}, f32[48,4096]{1,0:T(8,128)}) custom-call(bf16[2000,128]{1,0:T(8,128)(2,1)} %bitcast.2, bf16[384,4096]{1,0:T(8,128)(2,1)} %hid_hbm.1, f32[1,2000]{1,0:T(1,128)} %bitcast.3, s32[4]{0:T(128)} %qlen_ref.1, s32[4]{0:T(128)} %plen_ref.1, s32[4,8]{1,0:T(4,128)} %owner_ref.1, s32[4,8]{1,0:T(4,128)} %index_ref.1, ...), custom_call_target="tpu_custom_call" | custom-call | tf_op jit(solution)/shard_map/pallas_call | solution.py:413
  162.9 1.3 copy.12
  164.2 2.1 %copy.13 = f32[48,4096]{1,0:T(8,128)} copy(f32[48,4096]{1,0:T(8,128)} %get-tuple-element.5) | data formatting | bytes 1572864

commit v3 on v2

--- a/solution.py
+++ b/solution.py
@@ -41,9 +41,9 @@
 
 
 def kernel(
-    w_hbm, hid_hbm, bias_ref, qlen_ref, plen_ref, owner_ref, index_ref, teacher_ref,
+    w_hbm, hid_hbm, bias_hbm, qlen_hbm, plen_hbm, owner_hbm, index_hbm, teacher_hbm,
     margin_ref, out_ref,
-    wt, hid, bias_s, lg_f, rall, inv_ref, lgrad, sbuf, mt_ref, psum_part, ron, fs, fr, ns, nr,
+    wt, hid, bias_ref, qlen_ref, plen_ref, owner_ref, index_ref, teacher_ref, bias_s, lg_f, rall, inv_ref, lgrad, rhi, rlo, sbuf, mt_ref, psum_part, ron, fs, fr, ns, nr,
     ld_sem, rsend, rrecv, zsend, zrecv, ysend, yrecv, vsend, vrecv, osend, orecv, fsend, frecv, nsend, nrecv,
 ):
     dp = lax.axis_index("dp")
@@ -70,6 +70,17 @@
     ld_h = pltpu.make_async_copy(hid_hbm, hid, ld_sem.at[1])
     ld_w.start()
     ld_h.start()
+    small = [
+        pltpu.make_async_copy(src, dst, ld_sem.at[2 + i])
+        for i, (src, dst) in enumerate(
+            [
+                (bias_hbm, bias_ref), (qlen_hbm, qlen_ref), (plen_hbm, plen_ref),
+                (owner_hbm, owner_ref), (index_hbm, index_ref), (teacher_hbm, teacher_ref),
+            ]
+        )
+    ]
+    for cp in small:
+        cp.start()
 
     barrier = pltpu.get_barrier_semaphore()
     peers = [dp_dev(y_up, z), dp_dev(y_dn, z), dp_dev(y, z_up), dp_dev(y, z_dn)]
@@ -117,6 +128,8 @@
         return carry
 
     lax.fori_loop(0, NDP, clear, 0)
+    for cp in small:
+        cp.wait()
     bias_s[...] = jnp.zeros_like(bias_s)
     bias_s[:, 0:VW] = bias_ref[...]
     lg_f[...] = jnp.broadcast_to(bias_s[...], (TOK, VP))
@@ -189,11 +202,11 @@
             inv_ref[g : g + 1, cols] = 1.0 / (summed * SCALE)
         row0 += span
 
-    half = 1280
+    half = VP // 2
     h1 = pl.ds(0, half)
     h0 = pl.ds(half, RW - half)
-    far1 = (pl.ds(0, 640), pl.ds(640, half - 640))
-    far0 = (pl.ds(half, 384), pl.ds(half + 384, RW - half - 384))
+    far1 = (pl.ds(0, half // 2), pl.ds(half // 2, half // 2))
+    far0 = (pl.ds(half, 512), pl.ds(half + 512, RW - half - 512))
     sends = []
 
     def go(src, ss, rs, dev):
@@ -226,36 +239,24 @@
     def y_send(slot, zo, cols):
         go(rall.at[zo, y, :, cols], ysend.at[slot, 0], yrecv.at[slot, 0], dp_dev(y_up, z))
         go(rall.at[zo, y, :, cols], ysend.at[slot, 1], yrecv.at[slot, 1], dp_dev(y_dn, z))
+        go(rall.at[zo, y, :, cols], ysend.at[slot, 2], yrecv.at[slot, 2], dp_dev(rem(y + 2, NY), z))
 
     def y_wait(slot, way, zo, cols):
         ref = rall.at[zo, y_off[way + 1], :, cols]
         remote(ref, ref, ysend.at[slot, way], yrecv.at[slot, way], dp_dev(y_up, z)).wait_recv()
 
-    def y_relay(slot, zo, cols):
-        y_wait(slot, 0, zo, cols)
-        y_wait(slot, 1, zo, cols)
-        odd = rem(zo, 2)
-        src_y = rem(y + NY - 1 + 2 * odd, NY)
-        dst_y = rem(y + 1 + 2 * odd, NY)
-        go(rall.at[zo, src_y, :, cols], ysend.at[slot, 2], yrecv.at[slot, 2], dp_dev(dst_y, z))
-
     y_send(NZ, z, h0)
     for way in range(2):
+        z_send(NY, way, 1)
         z_send(0, way, 1)
-        z_send(NY, way, 1)
     y_send(0, z, h1)
-    y_relay(NZ, z, h0)
-    for way in range(2):
-        z_send(1, way, 1)
-        z_send(2, way, 1)
-    y_wait(NZ, 2, z, h0)
-    for way in range(2):
-        z_send(3, way, 1)
-    last = [(0, z)]
+    for j in range(1, NY):
+        y_wait(NZ, j - 1, z, h0)
+        for way in range(2):
+            z_send(j, way, 1)
     order = [(0, z)]
     for d in range(1, mid + 1):
-        fresh = []
-        for j in (0, NY, 1, 2, 3):
+        for j in (NY, 0, 1, 2, 3):
             for way in range(2):
                 z_wait(j, way, d)
                 if d < mid:
@@ -263,22 +264,21 @@
                 if j == NY and (d < mid or way == 1):
                     slot = 2 * d - 1 + way if d < mid else NZ - 1
                     y_send(slot, z_origin(way, d), h1)
-                    fresh.append((slot, z_origin(way, d)))
-            if j == 1:
-                for slot, zo in last:
-                    y_relay(slot, zo, h1)
-        last = fresh
-        order += fresh
-    for slot, zo in last:
-        y_relay(slot, zo, h1)
+                    order.append((slot, z_origin(way, d)))
     for slot, zo in order:
-        y_wait(slot, 2, zo, h1)
+        for way in range(3):
+            y_wait(slot, way, zo, h1)
 
     n_rows = NDP * 8
     reps = rall[:, :, :, 0:VP].reshape(n_rows, VP)
-    gram = lax.dot_general(
-        reps, reps, (((1,), (1,)), ((), ())), precision=HI, preferred_element_type=jnp.float32
-    )
+    high = reps.astype(jnp.bfloat16)
+    rhi[...] = high
+    rlo[...] = (reps - high.astype(jnp.float32)).astype(jnp.bfloat16)
+
+    def nt(p, q):
+        return lax.dot_general(p, q, (((1,), (1,)), ((), ())), preferred_element_type=jnp.float32)
+
+    gram = nt(rhi[...], rhi[...]) + (nt(rhi[...], rlo[...]) + nt(rlo[...], rhi[...]))
     meta = rall[:, :, :, META:].reshape(n_rows, 128)
     meta_t = meta.T
     row_id = lax.broadcasted_iota(jnp.int32, (n_rows, n_rows), 0).astype(jnp.float32)
@@ -316,9 +316,11 @@
     for k in range(NEG):
         coef = coef - jnp.where(sub_id == meta_t[k : k + 1, :], margin[k : k + 1, :], 0.0)
         coef = coef - jnp.where(lanes == meta_loc[:, k : k + 1], m_loc[:, k : k + 1], 0.0)
-    rep_grad = lax.dot_general(
-        coef, reps, (((1,), (0,)), ((), ())), precision=HI, preferred_element_type=jnp.float32
-    )
+    coef_hi = coef.astype(jnp.bfloat16).astype(jnp.float32)
+    both = jnp.concatenate([coef_hi, coef - coef_hi], axis=0).astype(jnp.bfloat16)
+    by_hi = jnp.dot(both, rhi[...], preferred_element_type=jnp.float32)
+    by_lo = jnp.dot(both, rlo[...], preferred_element_type=jnp.float32)
+    rep_grad = by_hi[0:8, :] + (by_hi[8:16, :] + by_lo[0:8, :])
     row0 = 0
     for g in range(2 * QD):
         span = LQ if g < QD else LP
@@ -416,25 +418,24 @@
             jax.ShapeDtypeStruct((QD, NEG), f32),
             jax.ShapeDtypeStruct((ROWS, D), f32),
         ),
-        in_specs=[
-            pl.BlockSpec(memory_space=pl.ANY),
-            pl.BlockSpec(memory_space=pl.ANY),
-            pl.BlockSpec(memory_space=pltpu.VMEM),
-            pl.BlockSpec(memory_space=pltpu.SMEM),
-            pl.BlockSpec(memory_space=pltpu.SMEM),
-            pl.BlockSpec(memory_space=pltpu.VMEM),
-            pl.BlockSpec(memory_space=pltpu.VMEM),
-            pl.BlockSpec(memory_space=pltpu.VMEM),
-        ],
+        in_specs=[pl.BlockSpec(memory_space=pl.ANY)] * 8,
         out_specs=(pl.BlockSpec(memory_space=pltpu.VMEM), pl.BlockSpec(memory_space=pltpu.VMEM)),
         scratch_shapes=[
             vm((NDP, VP, KB), bf16),
             vm((TOK, D), bf16),
+            vm((1, VW), f32),
+            pltpu.SMEM((QD,), jnp.int32),
+            pltpu.SMEM((QD,), jnp.int32),
+            vm((QD, NEG), jnp.int32),
+            vm((QD, NEG), jnp.int32),
+            vm((QD, NEG), f32),
             vm((1, VP), f32),
             vm((TOK, VP), f32),
             vm((NZ, NY, 8, RW), f32),
             vm((8, VP), f32),
             vm((TOK, VP), bf16),
+            vm((NDP * 8, VP), bf16),
+            vm((NDP * 8, VP), bf16),
             vm((2 * NX, 16, NDP * 8), f32),
             vm((NDP * 8, 128), f32),
             vm((NCH, 2, NX, ROWS, CH), f32),
@@ -443,7 +444,7 @@
             vm((NCH, 2, ROWS, CH // 2), bf16),
             vm((NCH, 2, ROWS, CH), bf16),
             vm((NCH, 2, ROWS, CH), bf16),
-            dma((2,)),
+            dma((8,)),
             dma((STREAMS, SUB)),
             dma((STREAMS, FAR, SUB)),
             dma((NY + 1, 2, NZ // 2)),

time: 166 us -> 159 us (0.958)
  Pallas kernels: 162 us -> 155 us
    pallas_call x1, Pallas kernels: 162 us -> 155 us  [per_device(): pl.pallas_call(kernel, out_shape=(jax.ShapeDtypeStruct((QD, NEG), f32), j...]
where the time goes in v3:
time: 159 us
  Pallas kernels  155 us (97%)
  local copies, waits for them, and re-layouts  3.32 us (2%)
    pallas_call x1, Pallas kernels, per_device(): pl.pallas_call(kernel, out_shape=(jax.ShapeDtypeStruct((QD, NEG), f32), j...  155 us
    unnamed x2, local copies, waits for them, and re-layouts  3.32 us

profile of v3, /device:TPU:1, one launch (start us, length us, event | category | flops | bytes accessed | tf_op | source)
XLA Modules:
  0.0 158.7 jit_solution(8846829365650054415)
XLA Ops:
  0.6 154.8 %shard_map.95 = (f32[4,8]{1,0:T(4,128)}, f32[48,4096]{1,0:T(8,128)}) custom-call(bf16[2000,128]{1,0:T(8,128)(2,1)} %bitcast.2, bf16[384,4096]{1,0:T(8,128)(2,1)} %hid_hbm.1, f32[1,2000]{1,0:T(1,128)} %bitcast.3, s32[4]{0:T(128)} %qlen_hbm.1, s32[4]{0:T(128)} %plen_hbm.1, s32[4,8]{1,0:T(4,128)} %owner_hbm.1, s32[4,8]{1,0:T(4,128)} %index_hbm.1, ...), custom_call_target="tpu_custom_call" | custom-call | tf_op jit(solution)/shard_map/pallas_call | solution.py:415
  155.4 1.3 copy.12
  156.7 2.1 %copy.13 = f32[48,4096]{1,0:T(8,128)} copy(f32[48,4096]{1,0:T(8,128)} %get-tuple-element.5) | data formatting | bytes 1572864

commit v4 on v3

--- a/solution.py
+++ b/solution.py
@@ -18,7 +18,8 @@
 STREAMS = 4
 CW = VP // STREAMS
 HW = VP // 2
-SUB = 4
+SUB = 2
+PER = STREAMS // SUB
 SR = HW // SUB
 FAR = NDP // 2
 META = VP
@@ -168,12 +169,13 @@
 
             @pl.when(s > 1)
             def _():
-                mm_after(sub, before)
+                for i in range(PER):
+                    mm_after(sub * PER + i, before)
 
         return tuple(org)
 
     before = lax.fori_loop(1, FAR, ring_body, (dp,) * STREAMS)
-    for sub in range(SUB):
+    for sub in range(STREAMS):
         mm_after(sub, before)
     for q in range(STREAMS):
         for sub in far_subs(q):
@@ -207,12 +209,9 @@
     h0 = pl.ds(half, RW - half)
     far1 = (pl.ds(0, half // 2), pl.ds(half // 2, half // 2))
     far0 = (pl.ds(half, 512), pl.ds(half + 512, RW - half - 512))
-    sends = []
 
     def go(src, ss, rs, dev):
-        cp = remote(src, src, ss, rs, dev)
-        cp.start()
-        sends.append(cp)
+        remote(src, src, ss, rs, dev).start()
 
     z_next = (dp_dev(y, z_up), dp_dev(y, z_dn))
     y_off = [y, y_dn, y_up, rem(y + 2, NY)]
@@ -226,24 +225,22 @@
             ref = rall.at[zo, y_off[j], :, far0[way] if d == mid else h0]
         else:
             ref = rall.at[zo, y, :, far1[way] if d == mid else h1]
-        return remote(ref, ref, zsend.at[j, way, d - 1], zrecv.at[j, way, d - 1], z_next[way])
+        return remote(ref, ref, zsend.at[j // NY], zrecv.at[j, way, d - 1], z_next[way])
 
     def z_send(j, way, d):
-        cp = z_copy(j, way, d, z_origin(way, d - 1))
-        cp.start()
-        sends.append(cp)
+        z_copy(j, way, d, z_origin(way, d - 1)).start()
 
     def z_wait(j, way, d):
         z_copy(j, way, d, z_origin(way, d)).wait_recv()
 
     def y_send(slot, zo, cols):
-        go(rall.at[zo, y, :, cols], ysend.at[slot, 0], yrecv.at[slot, 0], dp_dev(y_up, z))
-        go(rall.at[zo, y, :, cols], ysend.at[slot, 1], yrecv.at[slot, 1], dp_dev(y_dn, z))
-        go(rall.at[zo, y, :, cols], ysend.at[slot, 2], yrecv.at[slot, 2], dp_dev(rem(y + 2, NY), z))
+        go(rall.at[zo, y, :, cols], ysend.at[slot // NZ], yrecv.at[slot, 0], dp_dev(y_up, z))
+        go(rall.at[zo, y, :, cols], ysend.at[slot // NZ], yrecv.at[slot, 1], dp_dev(y_dn, z))
+        go(rall.at[zo, y, :, cols], ysend.at[slot // NZ], yrecv.at[slot, 2], dp_dev(rem(y + 2, NY), z))
 
     def y_wait(slot, way, zo, cols):
         ref = rall.at[zo, y_off[way + 1], :, cols]
-        remote(ref, ref, ysend.at[slot, way], yrecv.at[slot, way], dp_dev(y_up, z)).wait_recv()
+        remote(ref, ref, ysend.at[slot // NZ], yrecv.at[slot, way], dp_dev(y_up, z)).wait_recv()
 
     y_send(NZ, z, h0)
     for way in range(2):
@@ -290,10 +287,10 @@
     sbuf[v, NEG : NEG + 1, :] = jnp.sum(jnp.where(is_pos, gram, 0.0), axis=0, keepdims=True)
     sbuf[v, NEG + 1 :, :] = jnp.zeros((16 - NEG - 1, n_rows), jnp.float32)
     for i in range(1, 2 * NX):
-        go(sbuf.at[v], vsend.at[i - 1], vrecv.at[i - 1], {"vocab": rem(v + i, 2 * NX)})
+        go(sbuf.at[v], vsend.at[0], vrecv.at[i - 1], {"vocab": rem(v + i, 2 * NX)})
     for i in range(1, 2 * NX):
         ref = sbuf.at[rem(v + 2 * NX - i, 2 * NX)]
-        remote(ref, ref, vsend.at[i - 1], vrecv.at[i - 1], {"vocab": rem(v + i, 2 * NX)}).wait_recv()
+        remote(ref, ref, vsend.at[0], vrecv.at[i - 1], {"vocab": rem(v + i, 2 * NX)}).wait_recv()
     total = sbuf[0]
     for i in range(1, 2 * NX):
         total = total + sbuf[i]
@@ -331,16 +328,16 @@
     other = 1 - c
 
     def on_copy(n):
-        return remote(psum_part.at[n, other], ron.at[n], osend.at[n], orecv.at[n], v_dev(x, other))
+        return remote(psum_part.at[n, other], ron.at[n], osend.at[0], orecv.at[n], v_dev(x, other))
 
     def far_copy(n, way):
         return remote(
-            fs.at[n, way], fr.at[n, way], fsend.at[n, way], frecv.at[n, way], v_dev((x_up, x_dn)[way], c)
+            fs.at[n, way], fr.at[n, way], fsend.at[0], frecv.at[n, way], v_dev((x_up, x_dn)[way], c)
         )
 
     def near_copy(n, way):
         return remote(
-            ns.at[n, way], nr.at[n, way], nsend.at[n, way], nrecv.at[n, way], v_dev((x_up, x_dn)[way], c)
+            ns.at[n, way], nr.at[n, way], nsend.at[0], nrecv.at[n, way], v_dev((x_up, x_dn)[way], c)
         )
 
     hw = CH // 2
@@ -391,19 +388,23 @@
 
     lax.fori_loop(0, NCH + S4, bwd_body, 0)
 
-    for cp in sends:
-        cp.wait_send()
+    def sent_all(ref, ss, rs):
+        remote(ref, ref, ss, rs, v_dev(x, other)).wait_send()
+
+    sent_all(rall.at[0 : NZ - 1, :, :, h0], zsend.at[0], zrecv.at[0, 0, 0])
+    sent_all(rall.at[0 : NZ - 1, 0, :, h1], zsend.at[1], zrecv.at[0, 0, 0])
+    sent_all(rall.at[0 : 3 * NZ // NY, :, :, h1], ysend.at[0], yrecv.at[0, 0])
+    sent_all(rall.at[0, 0:3, :, h0], ysend.at[1], yrecv.at[0, 0])
+    sent_all(sbuf.at[0 : 2 * NX - 1], vsend.at[0], vrecv.at[0])
+    sent_all(ron, osend.at[0], orecv.at[0])
+    sent_all(fs, fsend.at[0], frecv.at[0, 0])
+    sent_all(ns, nsend.at[0], nrecv.at[0, 0])
 
     for q in range(STREAMS):
         for sub in range(SUB):
             steps = FAR if sub in far_subs(q) else FAR - 1
             sent = wt.at[0:steps, 0 : sub_rows(q, sub), :]
             remote(sent, sent, rsend.at[q, sub], rrecv.at[q, 0, sub], nxt[q]).wait_send()
-    for n in range(NCH):
-        on_copy(n).wait_send()
-        for way in range(2):
-            far_copy(n, way).wait_send()
-            near_copy(n, way).wait_send()
 
 
 def per_device(
@@ -447,17 +448,17 @@
             dma((8,)),
             dma((STREAMS, SUB)),
             dma((STREAMS, FAR, SUB)),
+            dma((2,)),
             dma((NY + 1, 2, NZ // 2)),
-            dma((NY + 1, 2, NZ // 2)),
+            dma((2,)),
             dma((NZ + 1, 3)),
-            dma((NZ + 1, 3)),
+            dma((1,)),
             dma((2 * NX - 1,)),
-            dma((2 * NX - 1,)),
+            dma((1,)),
             dma((NCH,)),
-            dma((NCH,)),
+            dma((1,)),
             dma((NCH, 2)),
-            dma((NCH, 2)),
-            dma((NCH, 2)),
+            dma((1,)),
             dma((NCH, 2)),
         ],
         compiler_params=pltpu.CompilerParams(

time: 159 us -> 157 us (0.987)
  Pallas kernels: 155 us -> 153 us
    pallas_call x1, Pallas kernels: 155 us -> 153 us  [per_device(): pl.pallas_call(kernel, out_shape=(jax.ShapeDtypeStruct((QD, NEG), f32), j...]
where the time goes in v4:
time: 157 us
  Pallas kernels  153 us (97%)
  local copies, waits for them, and re-layouts  3.32 us (2%)
    pallas_call x1, Pallas kernels, per_device(): pl.pallas_call(kernel, out_shape=(jax.ShapeDtypeStruct((QD, NEG), f32), j...  153 us
    unnamed x2, local copies, waits for them, and re-layouts  3.32 us

profile of v4, /device:TPU:1, one launch (start us, length us, event | category | flops | bytes accessed | tf_op | source)
XLA Modules:
  0.0 156.8 jit_solution(2083420375102217785)
XLA Ops:
  0.6 152.8 %shard_map.95 = (f32[4,8]{1,0:T(4,128)}, f32[48,4096]{1,0:T(8,128)}) custom-call(bf16[2000,128]{1,0:T(8,128)(2,1)} %bitcast.2, bf16[384,4096]{1,0:T(8,128)(2,1)} %hid_hbm.1, f32[1,2000]{1,0:T(1,128)} %bitcast.3, s32[4]{0:T(128)} %qlen_hbm.1, s32[4]{0:T(128)} %plen_hbm.1, s32[4,8]{1,0:T(4,128)} %owner_hbm.1, s32[4,8]{1,0:T(4,128)} %index_hbm.1, ...), custom_call_target="tpu_custom_call" | custom-call | tf_op jit(solution)/shard_map/pallas_call | solution.py:416
  153.5 1.3 copy.12
  154.7 2.1 %copy.13 = f32[48,4096]{1,0:T(8,128)} copy(f32[48,4096]{1,0:T(8,128)} %get-tuple-element.5) | data formatting | bytes 1572864

commit v5 on v4

--- a/solution.py
+++ b/solution.py
@@ -43,8 +43,8 @@
 
 def kernel(
     w_hbm, hid_hbm, bias_hbm, qlen_hbm, plen_hbm, owner_hbm, index_hbm, teacher_hbm,
-    margin_ref, out_ref,
-    wt, hid, bias_ref, qlen_ref, plen_ref, owner_ref, index_ref, teacher_ref, bias_s, lg_f, rall, inv_ref, lgrad, rhi, rlo, sbuf, mt_ref, psum_part, ron, fs, fr, ns, nr,
+    margin_ref, out_hbm,
+    wt, out_s, hid, bias_ref, qlen_ref, plen_ref, owner_ref, index_ref, teacher_ref, bias_s, lg_f, rall, inv_ref, lgrad, rhi, rlo, sbuf, mt_ref, psum_part, ron, fs, fr, ns, nr,
     ld_sem, rsend, rrecv, zsend, zrecv, ysend, yrecv, vsend, vrecv, osend, orecv, fsend, frecv, nsend, nrecv,
 ):
     dp = lax.axis_index("dp")
@@ -382,12 +382,14 @@
             near_copy(m, 0).wait_recv()
             near_copy(m, 1).wait_recv()
             cols = pl.ds(pl.multiple_of(m * CH, CH), CH)
-            out_ref[:, cols] = own + nr[m, 0].astype(jnp.float32) + nr[m, 1].astype(jnp.float32)
+            out_s[:, cols] = own + nr[m, 0].astype(jnp.float32) + nr[m, 1].astype(jnp.float32)
+            pltpu.make_async_copy(out_s.at[:, cols], out_hbm.at[:, cols], ld_sem.at[8]).start()
 
         return carry
 
     lax.fori_loop(0, NCH + S4, bwd_body, 0)
 
+    pltpu.make_async_copy(out_s, out_hbm, ld_sem.at[8]).wait()
     def sent_all(ref, ss, rs):
         remote(ref, ref, ss, rs, v_dev(x, other)).wait_send()
 
@@ -420,9 +422,10 @@
             jax.ShapeDtypeStruct((ROWS, D), f32),
         ),
         in_specs=[pl.BlockSpec(memory_space=pl.ANY)] * 8,
-        out_specs=(pl.BlockSpec(memory_space=pltpu.VMEM), pl.BlockSpec(memory_space=pltpu.VMEM)),
+        out_specs=(pl.BlockSpec(memory_space=pltpu.VMEM), pl.BlockSpec(memory_space=pl.ANY)),
         scratch_shapes=[
             vm((NDP, VP, KB), bf16),
+            vm((ROWS, D), f32),
             vm((TOK, D), bf16),
             vm((1, VW), f32),
             pltpu.SMEM((QD,), jnp.int32),
@@ -445,7 +448,7 @@
             vm((NCH, 2, ROWS, CH // 2), bf16),
             vm((NCH, 2, ROWS, CH), bf16),
             vm((NCH, 2, ROWS, CH), bf16),
-            dma((8,)),
+            dma((9,)),
             dma((STREAMS, SUB)),
             dma((STREAMS, FAR, SUB)),
             dma((2,)),

time: 157 us -> 157 us (level)
  no operation moved by 1% of the time
where the time goes in v5:
time: 157 us
  Pallas kernels  153 us (97%)
  local copies, waits for them, and re-layouts  3.32 us (2%)
    pallas_call x1, Pallas kernels, per_device(): pl.pallas_call(kernel, out_shape=(jax.ShapeDtypeStruct((QD, NEG), f32), j...  153 us
    unnamed x2, local copies, waits for them, and re-layouts  3.32 us

profile of v5, /device:TPU:1, one launch (start us, length us, event | category | flops | bytes accessed | tf_op | source)
XLA Modules:
  0.0 157.2 jit_solution(4202397757634534979)
XLA Ops:
  0.6 153.2 %shard_map.95 = (f32[4,8]{1,0:T(4,128)}, f32[48,4096]{1,0:T(8,128)}) custom-call(bf16[2000,128]{1,0:T(8,128)(2,1)} %bitcast.2, bf16[384,4096]{1,0:T(8,128)(2,1)} %hid_hbm.1, f32[1,2000]{1,0:T(1,128)} %bitcast.3, s32[4]{0:T(128)} %qlen_hbm.1, s32[4]{0:T(128)} %plen_hbm.1, s32[4,8]{1,0:T(4,128)} %owner_hbm.1, s32[4,8]{1,0:T(4,128)} %index_hbm.1, ...), custom_call_target="tpu_custom_call" | custom-call | tf_op jit(solution)/shard_map/pallas_call | solution.py:418
  153.9 1.3 copy.12
  155.1 2.1 %copy.13 = f32[48,4096]{1,0:T(8,128)} copy(f32[48,4096]{1,0:T(8,128)} %get-tuple-element.5) | data formatting | bytes 1572864
